TPU v7x, 256 devices: a whole 4x4x8 slice. The times are simulated.
256 devices in a mesh: kv: 2 (over core), seq: 128 (over z, y, x).
Axes of the slice: x: 4, y: 4, z: 8, core: 2. Of those that a mesh axis runs over, the one named last changes fastest.
Arguments:
- tokens: bfloat16 [32768, 4096], P(('seq', 'kv')), may hold values from -6 to 6
- gain: float32 [4096], replicated, may hold values from 0.25 to 1.75
- w_query: bfloat16 [4096, 4096], P(None, 'kv'), may hold values from -1 to 1
- w_key: bfloat16 [4096, 1024], P(None, 'kv'), may hold values from -4 to 4
- w_value: bfloat16 [4096, 1024], P(None, 'kv'), may hold values from -0.09375 to 0.09375
- w_out: bfloat16 [4096, 4096], P('kv'), may hold values from -0.09375 to 0.09375
- segment_ids: int32 [32768], replicated, may hold values from 0 to 32767, as said below
- page_table: int32 [256], P('seq'), may hold values from 0 to 1, as said below
Outputs:
- mixed: bfloat16 [32768, 4096], P(('seq', 'kv'))
- attn_out: bfloat16 [32768, 4096], P(('seq', 'kv'))
- page_pool: bfloat16 [256, 2, 8, 128, 128], P('seq', None, 'kv')
Inputs may be any that keep to these rules, and one draw needn't show every extreme that they name: `segment_ids`: never falls along the stream; tokens of one prompt share the position of its first token as id; every prompt has 1 to 2048 tokens; exactly two prompts have 2048 tokens, one in each half of the stream, each beginning inside a block of 256 tokens and not at its first token; every other prompt has fewer than 128 tokens; the last token of the stream is a prompt of its own. `page_table`: in each aligned block of 2 entries every value appears once.
All inputs are finite; a program needn't handle non-finite values.
Results may differ from a plain program's by a relative error of at most 0.0065.
The roundings to bfloat16 on the way count: a program that leaves them out, or rounds other values in their place, can miss the bound.
Values may be sent and summed in bfloat16 or wider, within the bound.
A program may use at most 192 MiB of HBM per device.

v0:
```python
from functools import partial

import jax
import jax.numpy as jnp
from jax import lax
from jax.sharding import PartitionSpec as P

HD = 128


norm_eps = 1e-05


def shifted(value, axis, steps):
    count = lax.axis_size(axis)
    leading, last = (max(0, -steps), min(count, count - steps))
    return lax.ppermute(value, axis, [(source, source + steps) for source in range(leading, last)])


def head_attention(inputs, masks, live, sparse):
    query_head, key_blocks, value_blocks = inputs
    block_count = key_blocks.shape[0]
    key_width = key_blocks.shape[1]
    score_scale = query_head.shape[-1] ** (-0.5)

    def block_scores(distance):
        scores = (
            jnp.einsum(
                "qgd,kd->gqk", query_head, key_blocks[distance], preferred_element_type=jnp.float32
            )
            * score_scale
        )
        return jnp.where(masks[distance][None], scores, -jnp.inf)

    pieces = [block_scores(0)]
    for distance in range(1, block_count):
        pieces.append(block_scores(distance))
    scores = jnp.concatenate(pieces, axis=2)
    row_peak = jnp.max(scores, axis=2, keepdims=True)
    weights = jnp.exp(scores - row_peak).astype(jnp.bfloat16)
    row_total = jnp.sum(weights, axis=2, dtype=jnp.float32)
    all_values = value_blocks.reshape(block_count * key_width, value_blocks.shape[-1])
    weighted = jnp.einsum("gqk,kd->qgd", weights, all_values, preferred_element_type=jnp.float32)
    return (weighted / row_total.T[:, :, None]).astype(jnp.bfloat16)


def shards(tokens, gain, w_query, w_key, w_value, w_out, segment_ids, page_table):
    tok_rows = tokens.shape[0]
    block_rows = tok_rows * lax.axis_size("kv")
    reach = min(8, lax.axis_size("seq") // 2 - 1)
    kv_local = w_key.shape[1] // HD
    q_local = w_query.shape[1] // HD
    group_size = q_local // kv_local
    wide_rows = tokens.astype(jnp.float32)
    normed = (
        wide_rows
        * lax.rsqrt(jnp.mean(wide_rows * wide_rows, axis=1, keepdims=True) + norm_eps)
        * gain
    ).astype(jnp.bfloat16)
    piece = lax.all_gather(normed, "kv", axis=0, tiled=True)
    projected = jnp.concatenate(
        [
            jnp.dot(piece, w_query, preferred_element_type=jnp.float32),
            jnp.dot(piece, w_key, preferred_element_type=jnp.float32),
            jnp.dot(piece, w_value, preferred_element_type=jnp.float32),
        ],
        axis=1,
    ).astype(jnp.bfloat16)
    query_cols = q_local * HD
    key_cols = kv_local * HD
    query = projected[:, :query_cols].reshape(block_rows, kv_local, group_size, HD)
    key_rows = projected[:, query_cols : query_cols + key_cols].reshape(block_rows, kv_local, HD)
    value_rows = projected[:, query_cols + key_cols :].reshape(block_rows, kv_local, HD)
    pair_rows = jnp.stack([key_rows, value_rows], axis=0)
    page_rows = page_table.shape[0]
    page_len = block_rows // page_rows
    pages = pair_rows.reshape(2, page_rows, page_len, kv_local, HD).transpose(1, 0, 3, 2, 4)
    page_pool = jnp.zeros_like(pages).at[page_table].set(pages)
    received = [pair_rows]
    carried = pair_rows
    for distance in range(1, reach + 1):
        carried = shifted(carried, "seq", 1)
        received.append(carried)
    stacked_pairs = jnp.stack(received, axis=1)
    seq_index = lax.axis_index("seq")
    query_segs = lax.dynamic_slice_in_dim(segment_ids, seq_index * block_rows, block_rows)
    lower = jnp.arange(block_rows)[None, :] <= jnp.arange(block_rows)[:, None]
    mask_list = []
    live_list = []
    for distance in range(reach + 1):
        source = jnp.maximum(seq_index - distance, 0)
        valid = seq_index - distance >= 0
        key_segs = lax.dynamic_slice_in_dim(segment_ids, source * block_rows, block_rows)
        same = (key_segs[None, :] == query_segs[:, None]) & valid
        if distance == 0:
            same = same & lower
            live_list.append(jnp.array(True))
        else:
            live_list.append(valid & (key_segs[block_rows - 1] == query_segs[0]))
        mask_list.append(same)
    masks = jnp.stack(mask_list)
    live = jnp.stack(live_list)
    heads_out = lax.map(
        partial(head_attention, masks=masks, live=live, sparse=False),
        (
            query.transpose(1, 0, 2, 3),
            stacked_pairs[0].transpose(2, 0, 1, 3),
            stacked_pairs[1].transpose(2, 0, 1, 3),
        ),
    )
    attention = heads_out.transpose(1, 0, 2, 3).reshape(block_rows, q_local * HD)
    summed = lax.psum(jnp.dot(attention, w_out, preferred_element_type=jnp.float32), "kv")
    branch = lax.dynamic_slice_in_dim(summed, lax.axis_index("kv") * tok_rows, tok_rows, 0)
    attn_out = branch.astype(jnp.bfloat16)
    mixed = (wide_rows + branch).astype(jnp.bfloat16)
    return (mixed, attn_out, page_pool)


def solution(mesh):
    in_specs = (
        P(("seq", "kv"), None),
        P(),
        P(None, "kv"),
        P(None, "kv"),
        P(None, "kv"),
        P("kv", None),
        P(),
        P("seq"),
    )
    out_specs = (P(("seq", "kv"), None), P(("seq", "kv"), None), P("seq", None, "kv", None, None))
    return jax.shard_map(shards, mesh=mesh, in_specs=in_specs, out_specs=out_specs, check_vma=False)
```

profile of v0, /device:TPU:1, one launch (start us, length us, event | category | flops | bytes accessed | tf_op | source)
XLA Modules:
  0.0 373.4 jit_solution(7717644761476916831)
XLA Ops:
  8.7 2.5 fusion.73
  11.3 20.5 %all-gather.2.cloned.1.call-done = bf16[256,4096]{1,0:T(8,128)(2,1)} async-done(((bf16[128,4096]{1,0:T(8,128)(2,1)}), bf16[256,4096]{1,0:T(8,128)(2,1)}) %all-gather.2.cloned.1.call-update) | async-done | bytes 2097168 | tf_op jit(solution)/shard_map/all_gather | solution.py:60
  31.9 4.1 %convolution_convert_fusion.2 = bf16[256,512]{1,0:T(8,128)(2,1)S(1)} fusion(bf16[256,4096]{1,0:T(8,128)(2,1)} %all-gather.2.cloned.1.call-done, bf16[4096,512]{1,0:T(8,128)(2,1)} %param.13), kind=kOutput, calls=%fused_computation.115 | convolution fusion | flops 1073872896 | bytes 6553600 | tf_op jit(solution)/shard_map/dot_general | solution.py:64
  36.1 4.1 %convolution_convert_fusion.1 = bf16[256,512]{1,0:T(8,128)(2,1)S(1)} fusion(bf16[256,4096]{1,0:T(8,128)(2,1)} %all-gather.2.cloned.1.call-done, bf16[4096,512]{1,0:T(8,128)(2,1)} %param.14), kind=kOutput, calls=%fused_computation.114 | convolution fusion | flops 1073872896 | bytes 6553600 | tf_op jit(solution)/shard_map/dot_general | solution.py:65
  40.3 2.9 collective-permute-start
  43.1 11.0 %collective-permute-done = bf16[2,256,4,128]{3,1,2,0:T(8,128)(2,1)S(1)} collective-permute-done((bf16[2,256,4,128]{3,1,2,0:T(8,128)(2,1)S(1)}, bf16[2,256,4,128]{3,1,2,0:T(8,128)(2,1)S(1)}, u32[]{:S(2)}, u32[]{:S(2)}) %collective-permute-start) | collective-permute-done | bytes 524320 | tf_op jit(solution)/shard_map/ppermute | solution.py:17
  54.1 4.1 %collective-permute-start.1 = (bf16[2,256,4,128]{3,1,2,0:T(8,128)(2,1)S(1)}, bf16[2,256,4,128]{3,1,2,0:T(8,128)(2,1)S(1)}, u32[]{:S(2)}, u32[]{:S(2)}) collective-permute-start(bf16[2,256,4,128]{3,1,2,0:T(8,128)(2,1)S(1)} %collective-permute-done), channel_id=1, source_target_pairs={{0,1},{1,2},{2,3},{3,4},{4,5},{5,6},{6,7},{7,8},{8,9},{9,10},{10,1... | collective-permute-start | bytes 1572872 | tf_op jit(solution)/shard_map/ppermute | solution.py:17
  58.3 10.2 %collective-permute-done.1 = bf16[2,256,4,128]{3,1,2,0:T(8,128)(2,1)S(1)} collective-permute-done((bf16[2,256,4,128]{3,1,2,0:T(8,128)(2,1)S(1)}, bf16[2,256,4,128]{3,1,2,0:T(8,128)(2,1)S(1)}, u32[]{:S(2)}, u32[]{:S(2)}) %collective-permute-start.1) | collective-permute-done | bytes 524320 | tf_op jit(solution)/shard_map/ppermute | solution.py:17
  68.4 4.1 %collective-permute-start.2 = (bf16[2,256,4,128]{3,1,2,0:T(8,128)(2,1)S(1)}, bf16[2,256,4,128]{3,1,2,0:T(8,128)(2,1)S(1)}, u32[]{:S(2)}, u32[]{:S(2)}) collective-permute-start(bf16[2,256,4,128]{3,1,2,0:T(8,128)(2,1)S(1)} %collective-permute-done.1), channel_id=1, source_target_pairs={{0,1},{1,2},{2,3},{3,4},{4,5},{5,6},{6,7},{7,8},{8,9},{9,10},{10,1... | collective-permute-start | bytes 1572872 | tf_op jit(solution)/shard_map/ppermute | solution.py:17
  72.6 9.3 %collective-permute-done.2 = bf16[2,256,4,128]{3,1,2,0:T(8,128)(2,1)S(1)} collective-permute-done((bf16[2,256,4,128]{3,1,2,0:T(8,128)(2,1)S(1)}, bf16[2,256,4,128]{3,1,2,0:T(8,128)(2,1)S(1)}, u32[]{:S(2)}, u32[]{:S(2)}) %collective-permute-start.2) | collective-permute-done | bytes 524320 | tf_op jit(solution)/shard_map/ppermute | solution.py:17
  82.7 4.1 %collective-permute-start.3 = (bf16[2,256,4,128]{3,1,2,0:T(8,128)(2,1)S(1)}, bf16[2,256,4,128]{3,1,2,0:T(8,128)(2,1)S(1)}, u32[]{:S(2)}, u32[]{:S(2)}) collective-permute-start(bf16[2,256,4,128]{3,1,2,0:T(8,128)(2,1)S(1)} %collective-permute-done.2), channel_id=1, source_target_pairs={{0,1},{1,2},{2,3},{3,4},{4,5},{5,6},{6,7},{7,8},{8,9},{9,10},{10,1... | collective-permute-start | bytes 1572872 | tf_op jit(solution)/shard_map/ppermute | solution.py:17
  86.8 8.4 %collective-permute-done.3 = bf16[2,256,4,128]{3,1,2,0:T(8,128)(2,1)S(1)} collective-permute-done((bf16[2,256,4,128]{3,1,2,0:T(8,128)(2,1)S(1)}, bf16[2,256,4,128]{3,1,2,0:T(8,128)(2,1)S(1)}, u32[]{:S(2)}, u32[]{:S(2)}) %collective-permute-start.3) | collective-permute-done | bytes 524320 | tf_op jit(solution)/shard_map/ppermute | solution.py:17
  95.2 4.9 %collective-permute-start.4 = (bf16[2,256,4,128]{3,1,2,0:T(8,128)(2,1)S(1)}, bf16[2,256,4,128]{3,1,2,0:T(8,128)(2,1)}, u32[]{:S(2)}, u32[]{:S(2)}) collective-permute-start(bf16[2,256,4,128]{3,1,2,0:T(8,128)(2,1)S(1)} %collective-permute-done.3), channel_id=1, source_target_pairs={{0,1},{1,2},{2,3},{3,4},{4,5},{5,6},{6,7},{7,8},{8,9},{9,10},{10,1... | collective-permute-start | bytes 1572872 | tf_op jit(solution)/shard_map/ppermute | solution.py:17
  101.3 5.7 %collective-permute-done.4 = bf16[2,256,4,128]{3,1,2,0:T(8,128)(2,1)} collective-permute-done((bf16[2,256,4,128]{3,1,2,0:T(8,128)(2,1)S(1)}, bf16[2,256,4,128]{3,1,2,0:T(8,128)(2,1)}, u32[]{:S(2)}, u32[]{:S(2)}) %collective-permute-start.4) | collective-permute-done | bytes 524320 | tf_op jit(solution)/shard_map/ppermute | solution.py:17
  107.0 5.8 %collective-permute-start.5 = (bf16[2,256,4,128]{3,1,2,0:T(8,128)(2,1)}, bf16[2,256,4,128]{3,1,2,0:T(8,128)(2,1)}, u32[]{:S(2)}, u32[]{:S(2)}) collective-permute-start(bf16[2,256,4,128]{3,1,2,0:T(8,128)(2,1)} %collective-permute-done.4), channel_id=1, source_target_pairs={{0,1},{1,2},{2,3},{3,4},{4,5},{5,6},{6,7},{7,8},{8,9},{9,10},{10,1... | collective-permute-start | bytes 1572872 | tf_op jit(solution)/shard_map/ppermute | solution.py:17
  112.8 10.9 %convolution_convert_fusion = bf16[256,2048]{1,0:T(8,128)(2,1)S(1)} fusion(bf16[256,4096]{1,0:T(8,128)(2,1)} %all-gather.2.cloned.1.call-done, bf16[4096,2048]{1,0:T(8,128)(2,1)} %param.12), kind=kOutput, calls=%fused_computation.106 | convolution fusion | flops 4295491584 | bytes 19922944 | tf_op jit(solution)/shard_map/dot_general | solution.py:63
  126.9 5.5 %collective-permute-start.6 = (bf16[2,256,4,128]{3,1,2,0:T(8,128)(2,1)}, bf16[2,256,4,128]{3,1,2,0:T(8,128)(2,1)S(1)}, u32[]{:S(2)}, u32[]{:S(2)}) collective-permute-start(bf16[2,256,4,128]{3,1,2,0:T(8,128)(2,1)} %collective-permute-done.5), channel_id=1, source_target_pairs={{0,1},{1,2},{2,3},{3,4},{4,5},{5,6},{6,7},{7,8},{8,9},{9,10},{10,1... | collective-permute-start | bytes 1572872 | tf_op jit(solution)/shard_map/ppermute | solution.py:17
  133.6 5.5 %collective-permute-done.6 = bf16[2,256,4,128]{3,1,2,0:T(8,128)(2,1)S(1)} collective-permute-done((bf16[2,256,4,128]{3,1,2,0:T(8,128)(2,1)}, bf16[2,256,4,128]{3,1,2,0:T(8,128)(2,1)S(1)}, u32[]{:S(2)}, u32[]{:S(2)}) %collective-permute-start.6) | collective-permute-done | bytes 524320 | tf_op jit(solution)/shard_map/ppermute | solution.py:17
  139.1 6.4 %collective-permute-start.7 = (bf16[2,256,4,128]{3,1,2,0:T(8,128)(2,1)S(1)}, bf16[2,256,4,128]{3,1,2,0:T(8,128)(2,1)S(1)}, u32[]{:S(2)}, u32[]{:S(2)}) collective-permute-start(bf16[2,256,4,128]{3,1,2,0:T(8,128)(2,1)S(1)} %collective-permute-done.6), channel_id=1, source_target_pairs={{0,1},{1,2},{2,3},{3,4},{4,5},{5,6},{6,7},{7,8},{8,9},{9,10},{10,1... | collective-permute-start | bytes 1572872 | tf_op jit(solution)/shard_map/ppermute | solution.py:17
  147.8 3.6 collective-permute-done.7
  153.2 120.6 %while.12 = (s32[]{:T(128)}, bf16[4,256,4,128]{1,3,2,0:T(8,128)(2,1)}, bf16[4,9,256,128]{3,2,1,0:T(8,128)(2,1)S(1)}, bf16[4,9,256,128]{3,2,1,0:T(8,128)(2,1)}, b...) while((s32[]{:T(128)}, ...), condition=%wide.region_12.13_spmd.clone.clone, body=%wide.region_1.12_spmd.clone.clone.sunk | while | flops 1230764032 | bytes 72335304 | solution.py:103
  153.8 2.3 fusion.107
  163.0 2.4 fusion.111
  169.9 2.3 fusion.114
  172.2 2.3 fusion.115
  174.6 5.1 %convert_reduce_fusion.2 = f32[4,256]{1,0:T(4,128)S(1)} fusion(f32[4,256,2304]{1,2,0:T(8,128)} %get-tuple-element.530, f32[4,256]{1,0:T(4,128)S(1)} %maximum_maximum_fusion.2), kind=kLoop, calls=%fused_computation.10.clone.1 | loop fusion | flops 9436160 | bytes 9445376 | tf_op jit(solution)/shard_map/while/body/eval_jaxpr/reduce_sum | solution.py:41
  180.9 2.4 fusion.116
  184.0 2.3 fusion.107
  193.1 2.4 fusion.111
  200.1 2.3 fusion.114
  202.4 2.3 fusion.115
  204.7 5.1 %convert_reduce_fusion.2 = f32[4,256]{1,0:T(4,128)S(1)} fusion(f32[4,256,2304]{1,2,0:T(8,128)} %get-tuple-element.530, f32[4,256]{1,0:T(4,128)S(1)} %maximum_maximum_fusion.2), kind=kLoop, calls=%fused_computation.10.clone.1 | loop fusion | flops 9436160 | bytes 9445376 | tf_op jit(solution)/shard_map/while/body/eval_jaxpr/reduce_sum | solution.py:41
  211.1 2.4 fusion.116
  214.1 2.3 fusion.107
  223.3 2.4 fusion.111
  230.2 2.3 fusion.114
  232.5 2.3 fusion.115
  234.9 5.1 %convert_reduce_fusion.2 = f32[4,256]{1,0:T(4,128)S(1)} fusion(f32[4,256,2304]{1,2,0:T(8,128)} %get-tuple-element.530, f32[4,256]{1,0:T(4,128)S(1)} %maximum_maximum_fusion.2), kind=kLoop, calls=%fused_computation.10.clone.1 | loop fusion | flops 9436160 | bytes 9445376 | tf_op jit(solution)/shard_map/while/body/eval_jaxpr/reduce_sum | solution.py:41
  241.2 2.4 fusion.116
  253.4 2.4 fusion.111
  260.4 2.3 fusion.114
  262.7 2.3 fusion.115
  265.0 5.1 %convert_reduce_fusion.2 = f32[4,256]{1,0:T(4,128)S(1)} fusion(f32[4,256,2304]{1,2,0:T(8,128)} %get-tuple-element.530, f32[4,256]{1,0:T(4,128)S(1)} %maximum_maximum_fusion.2), kind=kLoop, calls=%fused_computation.10.clone.1 | loop fusion | flops 9436160 | bytes 9445376 | tf_op jit(solution)/shard_map/while/body/eval_jaxpr/reduce_sum | solution.py:41
  271.4 2.4 fusion.116
  273.8 12.7 %fusion.85 = f32[256,4096]{1,0:T(8,128)} fusion(bf16[256,2048]{0,1:T(8,128)(2,1)} %bitcast.280, bf16[2048,4096]{1,0:T(8,128)(2,1)} %param.15), kind=kOutput, calls=%fused_computation.141 | convolution fusion | flops 4294967296 | bytes 22020096 | tf_op jit(solution)/shard_map/dot_general | solution.py:112
  287.7 73.3 %all-reduce.2.cloned.1.call-done = f32[256,4096]{1,0:T(8,128)} async-done(((f32[256,4096]{1,0:T(8,128)}), f32[256,4096]{1,0:T(8,128)}) %all-reduce.2.cloned.1.call-update) | async-done | bytes 4194320 | tf_op jit(solution)/shard_map/psum | solution.py:112
  361.1 2.7 dynamic-slice_convert_fusion
  363.7 2.8 fusion.74
  (92 shorter events, 69.0 us)
Async XLA Ops:
  7.2 24.7 %all-gather.2.cloned.1.call-start = ((), (), s32[]{:S(2)}) async-start(), calls=%async_computation | async-start | bytes 3145728 | tf_op jit(solution)/shard_map/all_gather | solution.py:60
  11.3 349.8 %all-reduce.2.cloned.1.call-start = ((), (), s32[]{:S(2)}) async-start(), calls=%async_computation.1 | async-start | bytes 8388608 | tf_op jit(solution)/shard_map/psum | solution.py:112
  40.3 13.9 %collective-permute-start = (bf16[2,256,4,128]{3,1,2,0:T(8,128)(2,1)S(1)}, bf16[2,256,4,128]{3,1,2,0:T(8,128)(2,1)S(1)}, u32[]{:S(2)}, u32[]{:S(2)}) collective-permute-start(bf16[2,256,4,128]{3,1,2,0:T(8,128)(2,1)S(1)} %copy_dynamic-update-slice_fusion), channel_id=1, source_target_pairs={{0,1},{1,2},{2,3},{3,4},{4,5},{5,6},{6,7},{7,8},{8,9},{9,10},{10,1... | collective-permute-start | bytes 1572872 | tf_op jit(solution)/shard_map/ppermute | solution.py:17
  54.1 52.8 %copy-start.4 = (bf16[2,256,4,128]{3,1,2,0:T(8,128)(2,1)}, bf16[2,256,4,128]{3,1,2,0:T(8,128)(2,1)S(1)}, u32[]{:S(2)}) copy-start(bf16[2,256,4,128]{3,1,2,0:T(8,128)(2,1)S(1)} %collective-permute-done) | copy-start | bytes 1572868
  54.1 14.3 %collective-permute-start.1 = (bf16[2,256,4,128]{3,1,2,0:T(8,128)(2,1)S(1)}, bf16[2,256,4,128]{3,1,2,0:T(8,128)(2,1)S(1)}, u32[]{:S(2)}, u32[]{:S(2)}) collective-permute-start(bf16[2,256,4,128]{3,1,2,0:T(8,128)(2,1)S(1)} %collective-permute-done), channel_id=1, source_target_pairs={{0,1},{1,2},{2,3},{3,4},{4,5},{5,6},{6,7},{7,8},{8,9},{9,10},{10,1... | collective-permute-start | bytes 1572872 | tf_op jit(solution)/shard_map/ppermute | solution.py:17
  68.4 38.5 %copy-start.3 = (bf16[2,256,4,128]{3,1,2,0:T(8,128)(2,1)}, bf16[2,256,4,128]{3,1,2,0:T(8,128)(2,1)S(1)}, u32[]{:S(2)}) copy-start(bf16[2,256,4,128]{3,1,2,0:T(8,128)(2,1)S(1)} %collective-permute-done.1) | copy-start | bytes 1572868
  68.4 13.4 %collective-permute-start.2 = (bf16[2,256,4,128]{3,1,2,0:T(8,128)(2,1)S(1)}, bf16[2,256,4,128]{3,1,2,0:T(8,128)(2,1)S(1)}, u32[]{:S(2)}, u32[]{:S(2)}) collective-permute-start(bf16[2,256,4,128]{3,1,2,0:T(8,128)(2,1)S(1)} %collective-permute-done.1), channel_id=1, source_target_pairs={{0,1},{1,2},{2,3},{3,4},{4,5},{5,6},{6,7},{7,8},{8,9},{9,10},{10,1... | collective-permute-start | bytes 1572872 | tf_op jit(solution)/shard_map/ppermute | solution.py:17
  81.9 0.8 copy-start.5
  82.7 12.6 %collective-permute-start.3 = (bf16[2,256,4,128]{3,1,2,0:T(8,128)(2,1)S(1)}, bf16[2,256,4,128]{3,1,2,0:T(8,128)(2,1)S(1)}, u32[]{:S(2)}, u32[]{:S(2)}) collective-permute-start(bf16[2,256,4,128]{3,1,2,0:T(8,128)(2,1)S(1)} %collective-permute-done.2), channel_id=1, source_target_pairs={{0,1},{1,2},{2,3},{3,4},{4,5},{5,6},{6,7},{7,8},{8,9},{9,10},{10,1... | collective-permute-start | bytes 1572872 | tf_op jit(solution)/shard_map/ppermute | solution.py:17
  95.2 17.5 %copy-start.7 = (bf16[2,256,4,128]{3,1,2,0:T(8,128)(2,1)}, bf16[2,256,4,128]{3,1,2,0:T(8,128)(2,1)S(1)}, u32[]{:S(2)}) copy-start(bf16[2,256,4,128]{3,1,2,0:T(8,128)(2,1)S(1)} %collective-permute-done.3) | copy-start | bytes 1572868
  95.2 11.7 %collective-permute-start.4 = (bf16[2,256,4,128]{3,1,2,0:T(8,128)(2,1)S(1)}, bf16[2,256,4,128]{3,1,2,0:T(8,128)(2,1)}, u32[]{:S(2)}, u32[]{:S(2)}) collective-permute-start(bf16[2,256,4,128]{3,1,2,0:T(8,128)(2,1)S(1)} %collective-permute-done.3), channel_id=1, source_target_pairs={{0,1},{1,2},{2,3},{3,4},{4,5},{5,6},{6,7},{7,8},{8,9},{9,10},{10,1... | collective-permute-start | bytes 1572872 | tf_op jit(solution)/shard_map/ppermute | solution.py:17
  107.0 19.9 %collective-permute-start.5 = (bf16[2,256,4,128]{3,1,2,0:T(8,128)(2,1)}, bf16[2,256,4,128]{3,1,2,0:T(8,128)(2,1)}, u32[]{:S(2)}, u32[]{:S(2)}) collective-permute-start(bf16[2,256,4,128]{3,1,2,0:T(8,128)(2,1)} %collective-permute-done.4), channel_id=1, source_target_pairs={{0,1},{1,2},{2,3},{3,4},{4,5},{5,6},{6,7},{7,8},{8,9},{9,10},{10,1... | collective-permute-start | bytes 1572872 | tf_op jit(solution)/shard_map/ppermute | solution.py:17
  124.4 9.0 %copy-start.6 = (bf16[2,256,4,128]{3,1,2,0:T(8,128)(2,1)S(1)}, bf16[2,256,4,128]{3,1,2,0:T(8,128)(2,1)}, u32[]{:S(2)}) copy-start(bf16[2,256,4,128]{3,1,2,0:T(8,128)(2,1)} %copy-done.5) | copy-start | bytes 1572868
  124.4 9.1 %copy-start.8 = (bf16[2,256,4,128]{3,1,2,0:T(8,128)(2,1)S(1)}, bf16[2,256,4,128]{3,1,2,0:T(8,128)(2,1)}, u32[]{:S(2)}) copy-start(bf16[2,256,4,128]{3,1,2,0:T(8,128)(2,1)} %copy-done.7) | copy-start | bytes 1572868
  126.9 12.2 %collective-permute-start.6 = (bf16[2,256,4,128]{3,1,2,0:T(8,128)(2,1)}, bf16[2,256,4,128]{3,1,2,0:T(8,128)(2,1)S(1)}, u32[]{:S(2)}, u32[]{:S(2)}) collective-permute-start(bf16[2,256,4,128]{3,1,2,0:T(8,128)(2,1)} %collective-permute-done.5), channel_id=1, source_target_pairs={{0,1},{1,2},{2,3},{3,4},{4,5},{5,6},{6,7},{7,8},{8,9},{9,10},{10,1... | collective-permute-start | bytes 1572872 | tf_op jit(solution)/shard_map/ppermute | solution.py:17
  139.1 12.3 %collective-permute-start.7 = (bf16[2,256,4,128]{3,1,2,0:T(8,128)(2,1)S(1)}, bf16[2,256,4,128]{3,1,2,0:T(8,128)(2,1)S(1)}, u32[]{:S(2)}, u32[]{:S(2)}) collective-permute-start(bf16[2,256,4,128]{3,1,2,0:T(8,128)(2,1)S(1)} %collective-permute-done.6), channel_id=1, source_target_pairs={{0,1},{1,2},{2,3},{3,4},{4,5},{5,6},{6,7},{7,8},{8,9},{9,10},{10,1... | collective-permute-start | bytes 1572872 | tf_op jit(solution)/shard_map/ppermute | solution.py:17
  174.6 6.4 %copy-start = (f32[4,256,2304]{1,2,0:T(8,128)S(1)}, f32[4,256,2304]{1,2,0:T(8,128)}, u32[]{:S(2)}) copy-start(f32[4,256,2304]{1,2,0:T(8,128)} %get-tuple-element.530) | copy-start | bytes 28311556 | tf_op jit(solution)/shard_map/while
  204.7 6.4 %copy-start = (f32[4,256,2304]{1,2,0:T(8,128)S(1)}, f32[4,256,2304]{1,2,0:T(8,128)}, u32[]{:S(2)}) copy-start(f32[4,256,2304]{1,2,0:T(8,128)} %get-tuple-element.530) | copy-start | bytes 28311556 | tf_op jit(solution)/shard_map/while
  234.9 6.4 %copy-start = (f32[4,256,2304]{1,2,0:T(8,128)S(1)}, f32[4,256,2304]{1,2,0:T(8,128)}, u32[]{:S(2)}) copy-start(f32[4,256,2304]{1,2,0:T(8,128)} %get-tuple-element.530) | copy-start | bytes 28311556 | tf_op jit(solution)/shard_map/while
  265.0 6.4 %copy-start = (f32[4,256,2304]{1,2,0:T(8,128)S(1)}, f32[4,256,2304]{1,2,0:T(8,128)}, u32[]{:S(2)}) copy-start(f32[4,256,2304]{1,2,0:T(8,128)} %get-tuple-element.530) | copy-start | bytes 28311556 | tf_op jit(solution)/shard_map/while
  273.8 12.7 %copy-start.9 = (s32[2]{0:T(128)S(1)}, s32[2]{0:T(128)}, u32[]{:S(2)}) copy-start(s32[2]{0:T(128)} %param.17) | copy-start | bytes 28
  286.5 77.2 %copy-start.1 = (bf16[128,4096]{1,0:T(8,128)(2,1)S(1)}, bf16[128,4096]{1,0:T(8,128)(2,1)}, u32[]{:S(2)}) copy-start(bf16[128,4096]{1,0:T(8,128)(2,1)} %param.10) | copy-start | bytes 3145732
  287.7 78.8 %copy-start.2 = (bf16[2,2,4,128,128]{4,3,2,1,0:T(8,128)(2,1)}, bf16[2,2,4,128,128]{4,3,2,1,0:T(8,128)(2,1)S(1)}, u32[]{:S(2)}) copy-start(bf16[2,2,4,128,128]{4,3,2,1,0:T(8,128)(2,1)S(1)} %scatter_fusion) | copy-start | bytes 1572868
Sparse Core Ops, SparseCore 0:
  11.4 20.4 all-gather.1
  286.6 74.3 all-reduce.1
where the time goes:
time: 375 us; the launch traced here: 373 us
  waiting for transfers between devices  148 us (39%)
  matrix products  124 us (33%)
  starting transfers between devices  37.9 us (10%)
  other arithmetic  29.6 us (8%)
  local copies, waits for them, and re-layouts  19.6 us (5%)
  between operations  14.3 us (4%)
    dot_general x36, matrix products, block_scores(): jnp.einsum('qgd,kd->gqk', query_head, key_blocks[distance], preferred_ele...  82.9 us
    psum x1, waiting for transfers between devices, shards(): lax.psum(jnp.dot(attention, w_out, preferred_element_type=jnp.float32), '...  73.3 us
    ppermute x8, waiting for transfers between devices, shifted(): lax.ppermute(value, axis, [(source, source + steps) for source in range(l...  53.6 us
    ppermute x8, starting transfers between devices, shifted(): lax.ppermute(value, axis, [(source, source + steps) for source in range(l...  37.8 us
    all_gather x1, waiting for transfers between devices, shards(): piece = lax.all_gather(normed, 'kv', axis=0, tiled=True)  20.5 us
    reduce_sum x4, other arithmetic, head_attention(): row_total = jnp.sum(weights, axis=2, dtype=jnp.float32)  20.3 us
    dot_general x1, matrix products, shards(): jnp.dot(attention, w_out, preferred_element_type=jnp.float32)  12.7 us
    dot_general x1, matrix products, shards(): jnp.dot(piece, w_query, preferred_element_type=jnp.float32)  10.9 us
  transfers between devices with their start and end apart: 10, of which 9 were waited for; matrix products, arithmetic and copies ran while one was open for 5% of the time, Pallas kernels for 0%

commit v1 on v0

v1 whole, which is shorter than its diff:
```python
import functools

import jax
import jax.numpy as jnp
from jax import lax
from jax.experimental import pallas as pl
from jax.experimental.pallas import tpu as pltpu
from jax.sharding import PartitionSpec as P

HD = 128
EPS = 1e-05
NEG = -1e30
REACH = 8
ROW = 4
C = 2
MESH = pl.DeviceIdType.MESH


def kernel(
    n_seq,
    tok_hbm, gain_ref, wq_hbm, wk_hbm, wv_hbm, wo_hbm, seg_ref,
    mixed_hbm, attn_hbm, pages_hbm,
    X, N, W, B, Q, ACC, L, M, MB, QS, A, PP, PR, O1, O2,
    wsem, tsem, txs, txr, ss, rs, ps, pr, osem, gsem,
):
    kv = lax.axis_index("kv")
    s = lax.axis_index("seq")
    other = 1 - kv
    x = lax.rem(s, ROW)
    base = s - x
    right = base + lax.rem(x + 1, ROW)
    left = base + lax.rem(x + ROW - 1, ROW)
    up = lax.rem(s + ROW, n_seq)
    down = lax.rem(s + n_seq - ROW, n_seq)
    f32, bf16 = jnp.float32, jnp.bfloat16

    def load(slot, src, sem):
        return pltpu.make_async_copy(src, W.at[slot], wsem.at[sem])

    loads = []
    for h in range(2):
        loads.append(load(h, wk_hbm.at[pl.ds(h * 2048, 2048), :], h))
    for h in range(2):
        loads.append(load(2 + h, wv_hbm.at[pl.ds(h * 2048, 2048), :], 2 + h))
    for c in range(4):
        for h in range(2):
            i = 4 + 2 * c + h
            loads.append(load(i, wq_hbm.at[pl.ds(h * 2048, 2048), pl.ds(c * 512, 512)], i))
    own_tok = pltpu.make_async_copy(tok_hbm, X.at[kv], tsem)
    own_tok.start()
    for cp in loads[:4]:
        cp.start()

    barrier = pltpu.get_barrier_semaphore()
    pl.semaphore_signal(barrier, inc=1, device_id={"kv": other, "seq": s}, device_id_type=MESH)
    for peer in (right, left, up, down):
        pl.semaphore_signal(barrier, inc=1, device_id={"kv": kv, "seq": peer}, device_id_type=MESH)
    pl.semaphore_wait(barrier, 5)

    swap = pltpu.make_async_remote_copy(
        src_ref=tok_hbm, dst_ref=X.at[kv], send_sem=txs, recv_sem=txr,
        device_id={"kv": other, "seq": s}, device_id_type=MESH,
    )
    swap.start()
    for cp in loads[4:]:
        cp.start()

    for r in range(2):
        row = seg_ref[pl.ds(2 * s + r, 1), :].astype(f32)
        QS[pl.ds(r * 128, 128), :] = jnp.broadcast_to(row, (128, 128)).T

    gain = gain_ref[...]

    def norm_half(h):
        def body(i, carry):
            v = X[h, pl.ds(i * 16, 16), :].astype(f32)
            ms = jnp.mean(v * v, axis=1, keepdims=True)
            N[pl.ds(h * 128 + i * 16, 16), :] = (v * lax.rsqrt(ms + EPS) * gain).astype(bf16)
            return carry

        lax.fori_loop(0, 8, body, 0)

    own_tok.wait()
    norm_half(kv)
    swap.wait_recv()
    norm_half(other)

    def project(slot):
        return (
            jnp.dot(N[:, 0:2048], W[slot], preferred_element_type=f32)
            + jnp.dot(N[:, 2048:4096], W[slot + 1], preferred_element_type=f32)
        ).astype(bf16)

    loads[0].wait()
    loads[1].wait()
    B[0, 0] = project(0)
    loads[2].wait()
    loads[3].wait()
    B[0, 1] = project(2)
    outs = [load(n, wo_hbm.at[:, pl.ds(n * 512, 512)], 12 + n) for n in range(8)]
    for n in range(4):
        outs[n].start()

    def item(idx, c, src, dst, peer):
        rows = pl.ds(c * (256 // C), 256 // C)
        return pltpu.make_async_remote_copy(
            src_ref=B.at[src, :, rows, :], dst_ref=B.at[dst, :, rows, :],
            send_sem=ss.at[idx, c], recv_sem=rs.at[dst, c],
            device_id={"kv": kv, "seq": peer}, device_id_type=MESH,
        )

    last = x == ROW - 1
    first = x == 0
    zero = x * 0

    def y1(c):
        return item(0, c, 0, 4, up)

    def y2(c):
        return item(1, c, 4, 8, up)

    def xp1(c):
        return item(2, c, jnp.where(last, 4, 0), 1, right)

    def xp5(c):
        return item(3, c, jnp.where(last, 8, 4), 5, right)

    def xp2(c):
        return item(4, c, jnp.where(last, 5, 1), 2, right)

    def xm3(c):
        return item(5, c, jnp.where(first, 0, 4), 3, left)

    def xm7(c):
        return item(6, c, jnp.where(first, 4, 8), 7, left)

    def xm6(c):
        return item(7, c, jnp.where(first, 3, 7), 6, left)

    arrive = {1: xp1, 2: xp2, 3: xm3, 4: y1, 5: xp5, 6: xm6, 7: xm7, 8: y2}

    def wait_arrival(d, c):
        arrive[d](c).wait_recv()

    rows_i = lax.broadcasted_iota(jnp.int32, (256, 128), 0)
    cols_i = lax.broadcasted_iota(jnp.int32, (256, 128), 1)

    def attend(d):
        sd = lax.rem(s + n_seq - d, n_seq)
        for r in range(2):
            krow = seg_ref[pl.ds(2 * sd + r, 1), :].astype(f32)
            krow = jnp.where(s >= d, krow, -1.0)
            same = QS[...] == krow
            if d == 0:
                same = same & (cols_i + r * 128 <= rows_i)
            MB[:, r * 128:(r + 1) * 128] = jnp.where(same, 0.0, NEG)

        def body(g, carry):
            lanes = pl.ds(pl.multiple_of(g * 128, 128), 128)
            k = B[d, 0, :, lanes]
            va = jnp.concatenate([B[d, 1, :, lanes], jnp.ones((256, 128), bf16)], axis=1)
            for h in range(4):
                rows = pl.ds(h * 256, 256)
                sc = lax.dot_general(
                    Q[g, rows, :], k, (((1,), (1,)), ((), ())), preferred_element_type=f32
                ) * (HD ** -0.5) + MB[...]
                top = jnp.max(sc, axis=1, keepdims=True)
                if d == 0:
                    w = jnp.exp(sc - top).astype(bf16)
                    pv = jnp.dot(w, va, preferred_element_type=f32)
                    M[g, rows, :] = jnp.broadcast_to(top, (256, 128))
                    ACC[g, rows, :] = pv[:, :128]
                    L[g, rows, :] = pv[:, 128:]
                else:
                    old = M[g, rows, :]
                    new = jnp.maximum(old, jnp.broadcast_to(top, (256, 128)))
                    w = jnp.exp(sc - jnp.concatenate([new, new], axis=1)).astype(bf16)
                    pv = jnp.dot(w, va, preferred_element_type=f32)
                    fade = jnp.exp(old - new)
                    M[g, rows, :] = new
                    ACC[g, rows, :] = ACC[g, rows, :] * fade + pv[:, :128]
                    L[g, rows, :] = L[g, rows, :] * fade + pv[:, 128:]
            return carry

        lax.fori_loop(0, 4, body, 0)

    def query(c):
        loads[4 + 2 * c].wait()
        loads[5 + 2 * c].wait()
        q = project(4 + 2 * c)
        for h in range(4):
            Q[c, h * 256:(h + 1) * 256, :] = q[:, h * 128:(h + 1) * 128]

    for c in range(C):
        y1(c).start()

    @pl.when(x < ROW - 1)
    def _():
        for c in range(C):
            xp1(c).start()

    @pl.when(first)
    def _():
        for c in range(C):
            xm3(c).start()

    page_copies = []
    for p in range(2):
        for t in range(2):
            for g in range(4):
                i = (p * 2 + t) * 4 + g
                page_copies.append(pltpu.make_async_copy(
                    B.at[0, t, pl.ds(p * 128, 128), pl.ds(g * 128, 128)],
                    pages_hbm.at[p, t, g], gsem.at[i]))
    for cp in page_copies:
        cp.start()

    query(0)
    query(1)
    for n in range(4, 8):
        outs[n].start()
    for c in range(C):
        wait_arrival(4, c)
        y2(c).start()

        @pl.when(last)
        def _():
            xp1(c).start()

        @pl.when(x > 0)
        def _():
            xm3(c).start()

        if c == 0:
            query(2)

    @pl.when(x < ROW - 1)
    def _():
        for c in range(C):
            xp5(c).start()

    @pl.when(first)
    def _():
        for c in range(C):
            xm7(c).start()

    query(3)
    attend(0)
    for c in range(C):
        wait_arrival(1, c)
    for c in range(C):
        wait_arrival(3, c)
    attend(4)

    for c in range(C):
        wait_arrival(8, c)

        @pl.when(last)
        def _():
            xp5(c).start()

        @pl.when(x > 0)
        def _():
            xm7(c).start()

    @pl.when(x < ROW - 1)
    def _():
        for c in range(C):
            xp2(c).start()

    @pl.when(first)
    def _():
        for c in range(C):
            xm6(c).start()

    attend(1)
    for c in range(C):
        wait_arrival(5, c)

        @pl.when(last)
        def _():
            xp2(c).start()

        wait_arrival(7, c)

        @pl.when(x > 0)
        def _():
            xm6(c).start()

    attend(3)
    attend(8)
    attend(5)
    attend(7)
    for c in range(C):
        wait_arrival(2, c)
    attend(2)
    for c in range(C):
        wait_arrival(6, c)
    attend(6)

    for g in range(4):
        for h in range(4):
            rows = pl.ds(h * 256, 256)
            i = (g * 4 + h) * 128
            A[:, i:i + 128] = (ACC[g, rows, :] / L[g, rows, :]).astype(bf16)

    def give(n):
        return pltpu.make_async_remote_copy(
            src_ref=PP.at[n, other], dst_ref=PR.at[n], send_sem=ps.at[n], recv_sem=pr.at[n],
            device_id={"kv": other, "seq": s}, device_id_type=MESH,
        )

    def put(n):
        cols = pl.ds(n * 512, 512)
        return (
            pltpu.make_async_copy(O1.at[:, cols], attn_hbm.at[:, cols], osem.at[0, n]),
            pltpu.make_async_copy(O2.at[:, cols], mixed_hbm.at[:, cols], osem.at[1, n]),
        )

    def finish(n):
        give(n).wait_recv()
        cols = pl.ds(n * 512, 512)
        y = PP[n, kv] + PR[n]
        O1[:, cols] = y.astype(bf16)
        O2[:, cols] = (X[kv, :, cols].astype(f32) + y).astype(bf16)
        for cp in put(n):
            cp.start()

    for n in range(8):
        outs[n].wait()
        part = jnp.dot(A[...], W[n], preferred_element_type=f32)
        PP[n, 0] = part[:128]
        PP[n, 1] = part[128:]
        give(n).start()
        if n >= 2:
            finish(n - 2)
    finish(6)
    finish(7)

    swap.wait_send()
    for c in range(C):
        for f in arrive.values():
            f(c).wait_send()
    for n in range(8):
        give(n).wait_send()
        for cp in put(n):
            cp.wait()
    for cp in page_copies:
        cp.wait()


def shards(n_seq, tokens, gain, w_query, w_key, w_value, w_out, segment_ids, page_table):
    bf16, f32 = jnp.bfloat16, jnp.float32
    any_spec = pl.BlockSpec(memory_space=pl.ANY)
    vmem_spec = pl.BlockSpec(memory_space=pltpu.VMEM)
    dma = pltpu.SemaphoreType.DMA
    mixed, attn_out, pages = pl.pallas_call(
        functools.partial(kernel, n_seq),
        out_shape=(
            jax.ShapeDtypeStruct((128, 4096), bf16),
            jax.ShapeDtypeStruct((128, 4096), bf16),
            jax.ShapeDtypeStruct((2, 2, 4, 128, 128), bf16),
        ),
        in_specs=[any_spec, vmem_spec, any_spec, any_spec, any_spec, any_spec, vmem_spec],
        out_specs=(any_spec, any_spec, any_spec),
        scratch_shapes=[
            pltpu.VMEM((2, 128, 4096), bf16),
            pltpu.VMEM((256, 4096), bf16),
            pltpu.VMEM((12, 2048, 512), bf16),
            pltpu.VMEM((REACH + 1, 2, 256, 512), bf16),
            pltpu.VMEM((4, 1024, 128), bf16),
            pltpu.VMEM((4, 1024, 128), f32),
            pltpu.VMEM((4, 1024, 128), f32),
            pltpu.VMEM((4, 1024, 128), f32),
            pltpu.VMEM((256, 256), f32),
            pltpu.VMEM((256, 128), f32),
            pltpu.VMEM((256, 2048), bf16),
            pltpu.VMEM((8, 2, 128, 512), f32),
            pltpu.VMEM((8, 128, 512), f32),
            pltpu.VMEM((128, 4096), bf16),
            pltpu.VMEM((128, 4096), bf16),
            dma((20,)), dma, dma, dma,
            dma((8, C)), dma((REACH + 1, C)),
            dma((8,)), dma((8,)), dma((2, 8)), dma((16,)),
        ],
        compiler_params=pltpu.CompilerParams(
            collective_id=0, has_side_effects=True, vmem_limit_bytes=60 * 1024 * 1024
        ),
    )(tokens, gain.reshape(1, 4096), w_query, w_key, w_value, w_out, segment_ids.reshape(256, 128))
    page_pool = jnp.where(page_table[0] == 0, pages, pages[::-1])
    return mixed, attn_out, page_pool


def solution(mesh):
    in_specs = (
        P(("seq", "kv"), None),
        P(),
        P(None, "kv"),
        P(None, "kv"),
        P(None, "kv"),
        P("kv", None),
        P(),
        P("seq"),
    )
    out_specs = (P(("seq", "kv"), None), P(("seq", "kv"), None), P("seq", None, "kv", None, None))
    return jax.shard_map(
        functools.partial(shards, mesh.shape["seq"]),
        mesh=mesh, in_specs=in_specs, out_specs=out_specs, check_vma=False,
    )
```

time: 375 us -> 87.1 us (0.23)
  waiting for transfers between devices: 148 us -> 0 us
  matrix products: 124 us -> 0 us
  Pallas kernels: 0 us -> 79.5 us
  starting transfers between devices: 37.9 us -> 0 us
  other arithmetic: 29.6 us -> 2.14 us
  local copies, waits for them, and re-layouts: 19.6 us -> 4.58 us
  between operations: 14.3 us -> 0.69 us
    dot_general x44 -> x0, matrix products: 124 us -> none  [the longest x36 82.9 us: block_scores(): jnp.einsum('qgd,kd->gqk', query_head, key_blocks[distance], preferred_ele...]
    pallas_call x0 -> x1, Pallas kernels: none -> 79.5 us  [shards(): pl.pallas_call(functools.partial(kernel, n_seq), out_shape=(jax.ShapeDtyp...]
    psum x1 -> x0, waiting for transfers between devices: 73.3 us -> none  [shards(): lax.psum(jnp.dot(attention, w_out, preferred_element_type=jnp.float32), '...]
    ppermute x8 -> x0, waiting for transfers between devices: 53.6 us -> none  [shifted(): lax.ppermute(value, axis, [(source, source + steps) for source in range(l...]
    ppermute x8 -> x0, starting transfers between devices: 37.8 us -> none  [shifted(): lax.ppermute(value, axis, [(source, source + steps) for source in range(l...]
    reduce_sum x5 -> x0, other arithmetic: 21.8 us -> none  [the longest x4 20.3 us: head_attention(): row_total = jnp.sum(weights, axis=2, dtype=jnp.float32)]
    all_gather x1 -> x0, waiting for transfers between devices: 20.5 us -> none  [shards(): piece = lax.all_gather(normed, 'kv', axis=0, tiled=True)]
    convert_element_type x2 -> x0, other arithmetic: 5.3 us -> none  [the longest x1 2.77 us: shards(): mixed = (wide_rows + branch).astype(jnp.bfloat16)]
  transfers between devices with their start and end apart: 10 -> 0, of which waited for: 9 -> 0; matrix products, arithmetic and copies ran while one was open for 5% -> 0% of each run, Pallas kernels for 0% -> 0%
where the time goes in v1:
time: 87.1 us; the launch traced here: 86.9 us
  Pallas kernels  79.5 us (91%)
  local copies, waits for them, and re-layouts  4.58 us (5%)
  other arithmetic  2.14 us (2%)
    pallas_call x1, Pallas kernels, shards(): pl.pallas_call(functools.partial(kernel, n_seq), out_shape=(jax.ShapeDtyp...  79.5 us
    unnamed x4, local copies, waits for them, and re-layouts  4.58 us
    select_n x1, other arithmetic, shards(): page_pool = jnp.where(page_table[0] == 0, pages, pages[::-1])  2.14 us

profile of v1, /device:TPU:1, one launch (start us, length us, event | category | flops | bytes accessed | tf_op | source)
XLA Modules:
  0.0 86.9 jit_solution(10509234086967379854)
XLA Ops:
  0.6 0.0 copy-start
  0.6 79.5 %shard_map.103 = (bf16[128,4096]{1,0:T(8,128)(2,1)}, bf16[128,4096]{1,0:T(8,128)(2,1)}, bf16[2,2,4,128,128]{4,3,2,1,0:T(8,128)(2,1)}) custom-call(bf16[128,4096]{1,0:T(8,128)(2,1)} %tok_hbm.1, f32[1,4096]{1,0:T(1,128)} %bitcast.5, bf16[4096,2048]{1,0:T(8,128)(2,1)} %wq_hbm.1, bf16[4096,512]{1,0:T(8,128)(2,1)} %wk_hbm.1, bf16[4096,512]{1,0:T(8,128)(2,1)} %wv_hbm.1, ...), custom_call_target="tpu_custom_call" | custom-call | tf_op jit(solution)/shard_map/pallas_call | solution.py:357
  80.2 0.0 copy-done
  80.2 2.1 %reverse_select_fusion = bf16[2,2,4,128,128]{4,3,2,1,0:T(8,128)(2,1)} fusion(bf16[2,2,4,128,128]{4,3,2,1,0:T(8,128)(2,1)} %get-tuple-element.8, pred[]{:T(512)} %bitcast.2), kind=kLoop, calls=%fused_computation | loop fusion | flops 262144 | bytes 1048577 | tf_op jit(solution)/shard_map/jit(_where)/select_n | solution.py:390
  82.3 2.3 %copy.13 = bf16[128,4096]{1,0:T(8,128)(2,1)} copy(bf16[128,4096]{1,0:T(8,128)(2,1)} %get-tuple-element.12) | data formatting | bytes 2097152
  84.6 2.3 %copy.14 = bf16[128,4096]{1,0:T(8,128)(2,1)} copy(bf16[128,4096]{1,0:T(8,128)(2,1)} %get-tuple-element.13) | data formatting | bytes 2097152
Async XLA Ops:
  0.6 79.5 %copy-start = (s32[2]{0:T(128)S(1)}, s32[2]{0:T(128)}, u32[]{:S(2)}) copy-start(s32[2]{0:T(128)} %param.15) | copy-start | bytes 28

commit v2 on v1

v2 whole, which is shorter than its diff:
```python
import functools

import jax
import jax.numpy as jnp
from jax import lax
from jax.experimental import pallas as pl
from jax.experimental.pallas import tpu as pltpu
from jax.sharding import PartitionSpec as P

HD = 128
EPS = 1e-05
NEG = -1e30
REACH = 8
ROW = 4
MESH = pl.DeviceIdType.MESH


def kernel(
    n_seq,
    tok_hbm, gain_ref, wq_hbm, wk_hbm, wv_hbm, wo_hbm, seg_ref,
    mixed_ref, attn_ref, pages_ref,
    X, N, W, B, Q, ACC, L, M, MB, QS, QA, KA, PP, PR,
    wsem, tsem, txs, txr, ss, rs, ps, pr, gsem,
):
    kv = lax.axis_index("kv")
    s = lax.axis_index("seq")
    other = 1 - kv
    x = lax.rem(s, ROW)
    base = s - x
    right = base + lax.rem(x + 1, ROW)
    left = base + lax.rem(x + ROW - 1, ROW)
    up = lax.rem(s + ROW, n_seq)
    down = lax.rem(s + n_seq - ROW, n_seq)
    first = x == 0
    last = x == ROW - 1
    f32, bf16 = jnp.float32, jnp.bfloat16

    def load(i, src):
        return pltpu.make_async_copy(src, W.at[i], wsem.at[i])

    loads = []
    for w_hbm in (wk_hbm, wv_hbm):
        for h in range(2):
            loads.append(load(len(loads), w_hbm.at[pl.ds(h * 2048, 2048), :]))
    for c in range(4):
        for h in range(2):
            loads.append(load(
                len(loads), wq_hbm.at[pl.ds(h * 2048, 2048), pl.ds(c * 512, 512)]))

    def load_out(g, n):
        return pltpu.make_async_copy(
            wo_hbm.at[pl.ds(g * 512, 512), pl.ds(n * 512, 512)],
            W.at[2 * g + n // 4, pl.ds((n % 4) * 512, 512), :],
            wsem.at[12 + g * 8 + n])

    own_tok = pltpu.make_async_copy(tok_hbm, X.at[kv], tsem)
    own_tok.start()
    for cp in loads[:4]:
        cp.start()

    barrier = pltpu.get_barrier_semaphore()
    pl.semaphore_signal(barrier, inc=1, device_id={"kv": other, "seq": s}, device_id_type=MESH)
    for peer in (right, left, up, down):
        pl.semaphore_signal(barrier, inc=1, device_id={"kv": kv, "seq": peer}, device_id_type=MESH)
    pl.semaphore_wait(barrier, 5)

    swap = pltpu.make_async_remote_copy(
        src_ref=tok_hbm, dst_ref=X.at[kv], send_sem=txs, recv_sem=txr,
        device_id={"kv": other, "seq": s}, device_id_type=MESH,
    )
    swap.start()
    for cp in loads[4:]:
        cp.start()

    def clear(n, carry):
        PP[n] = jnp.zeros((2, 128, 512), f32)
        return carry

    lax.fori_loop(0, 8, clear, 0)
    gain = gain_ref[...]

    def norm_half(h):
        def body(i, carry):
            v = X[h, pl.ds(i * 16, 16), :].astype(f32)
            ms = jnp.mean(v * v, axis=1, keepdims=True)
            N[pl.ds(h * 128 + i * 16, 16), :] = (v * lax.rsqrt(ms + EPS) * gain).astype(bf16)
            return carry

        lax.fori_loop(0, 8, body, 0)

    own_tok.wait()
    norm_half(kv)

    def column(block, r):
        row = seg_ref[pl.ds(2 * block + r, 1), :].astype(f32)
        return jnp.broadcast_to(row, (128, 128)).T

    lane = lax.broadcasted_iota(jnp.int32, (128, 128), 1)
    opening = seg_ref[pl.ds(2 * s, 1), :].astype(f32)[:, :1]
    for r in range(2):
        rows = pl.ds(r * 128, 128)
        own = column(s, r)
        QS[rows, :] = own
        out = jnp.where(own == opening, 0.0, NEG)
        QA[rows, :] = jnp.where(lane == 0, out, jnp.where(lane == 1, 1.0, 0.0)).astype(bf16)

    def key_mask(d, carry):
        block = lax.rem(s + n_seq - d, n_seq)
        for r in range(2):
            out = jnp.where((column(block, r) == opening) & (s >= d), 0.0, NEG)
            KA[d, pl.ds(r * 128, 128), :] = jnp.where(
                lane == 1, out, jnp.where(lane == 0, 1.0, 0.0)).astype(bf16)
        return carry

    lax.fori_loop(1, REACH + 1, key_mask, 0)
    swap.wait_recv()
    norm_half(other)

    def project(slot):
        return (
            jnp.dot(N[:, 0:2048], W[slot], preferred_element_type=f32)
            + jnp.dot(N[:, 2048:4096], W[slot + 1], preferred_element_type=f32)
        ).astype(bf16)

    for t in range(2):
        loads[2 * t].wait()
        loads[2 * t + 1].wait()
        rows = project(2 * t)
        for g in range(4):
            B[0, g, t] = rows[:, g * 128:(g + 1) * 128]

    def item(idx, g, src, dst, peer):
        return pltpu.make_async_remote_copy(
            src_ref=B.at[src, g], dst_ref=B.at[dst, g],
            send_sem=ss.at[idx, g], recv_sem=rs.at[dst, g],
            device_id={"kv": kv, "seq": peer}, device_id_type=MESH,
        )

    def y4(g):
        return item(0, g, 0, 4, up)

    def y8(g):
        return item(1, g, 4, 8, up)

    def x1(g):
        return item(2, g, jnp.where(last, 4, 0), 1, right)

    def x5(g):
        return item(3, g, jnp.where(last, 8, 4), 5, right)

    def y5(g):
        return item(3, g, 1, 5, up)

    def x2(g):
        return item(4, g, jnp.where(last, 5, 1), 2, right)

    def x3(g):
        return item(5, g, jnp.where(first, 0, 4), 3, left)

    def x7(g):
        return item(6, g, jnp.where(first, 4, 8), 7, left)

    def x6(g):
        return item(7, g, jnp.where(first, 3, 7), 6, left)

    def y6(g):
        return item(7, g, 2, 6, up)

    relay = {1: x1, 2: x2, 3: x3, 4: y4, 5: x5, 6: x6, 7: x7, 8: y8}

    def arrived(d, g):
        relay[d](g).wait_recv()

    def send(cond, d, g):
        @pl.when(cond)
        def _():
            relay[d](g).start()

    for g in range(4):
        y4(g).start()
        send(x < ROW - 1, 1, g)
        send(first, 3, g)

    page_copies = []
    for p in range(2):
        for t in range(2):
            for g in range(4):
                page_copies.append(pltpu.make_async_copy(
                    B.at[0, g, t, pl.ds(p * 128, 128), :], pages_ref.at[p, t, g],
                    gsem.at[len(page_copies)]))
    for cp in page_copies:
        cp.start()

    def start_out(g):
        for n in range(8):
            load_out(g, n).start()

    def query(c):
        loads[4 + 2 * c].wait()
        loads[5 + 2 * c].wait()
        q = project(4 + 2 * c)
        for h in range(4):
            Q[c, h * 256:(h + 1) * 256, :] = q[:, h * 128:(h + 1) * 128]

    unit = HD ** -0.5 * 1.4426950408889634
    over = (((1,), (1,)), ((), ()))
    ones = jnp.ones((256, 128), bf16)

    def wide(v, n):
        return jnp.concatenate([v] * n, axis=1)

    def own_mask():
        rows_i = lax.broadcasted_iota(jnp.int32, (256, 128), 0)
        cols_i = lax.broadcasted_iota(jnp.int32, (256, 128), 1)
        for r in range(2):
            krow = seg_ref[pl.ds(2 * s + r, 1), :].astype(f32)
            same = (QS[...] == krow) & (cols_i + r * 128 <= rows_i)
            MB[:, r * 128:(r + 1) * 128] = jnp.where(same, 0.0, NEG)

    def attend_own(g):
        va = jnp.concatenate([B[0, g, 1], ones], axis=1)
        for h in range(4):
            rows = pl.ds(h * 256, 256)
            sc = lax.dot_general(
                Q[g, rows, :], B[0, g, 0], over, preferred_element_type=f32
            ) * unit + MB[...]
            top = jnp.broadcast_to(jnp.max(sc, axis=1, keepdims=True), (256, 128))
            w = jnp.exp2(sc - wide(top, 2)).astype(bf16)
            pv = jnp.dot(w, va, preferred_element_type=f32)
            M[g, rows, :] = top
            ACC[g, rows, :] = pv[:, :128]
            L[g, rows, :] = pv[:, 128:]

    def attend(d, e, g):
        k = jnp.concatenate([
            jnp.concatenate([B[d, g, 0], KA[d]], axis=1),
            jnp.concatenate([B[e, g, 0], KA[e]], axis=1)], axis=0)
        va = jnp.concatenate([
            jnp.concatenate([B[d, g, 1], ones], axis=1),
            jnp.concatenate([B[e, g, 1], ones], axis=1)], axis=0)
        for h in range(4):
            rows = pl.ds(h * 256, 256)
            q = jnp.concatenate([Q[g, rows, :], QA[...]], axis=1)
            sc = lax.dot_general(q, k, over, preferred_element_type=f32) * unit
            top = jnp.broadcast_to(jnp.max(sc, axis=1, keepdims=True), (256, 128))
            old = M[g, rows, :]
            new = jnp.maximum(old, top)
            w = jnp.exp2(sc - wide(new, 4)).astype(bf16)
            pv = jnp.dot(w, va, preferred_element_type=f32)
            fade = jnp.exp2(old - new)
            M[g, rows, :] = new
            ACC[g, rows, :] = ACC[g, rows, :] * fade + pv[:, :128]
            L[g, rows, :] = L[g, rows, :] * fade + pv[:, 128:]

    query(0)
    for g in range(4):
        arrived(4, g)
        y8(g).start()
        send(last, 1, g)
        send(x > 0, 3, g)
        if g < 3:
            send(x < ROW - 1, 5, g)
        send(first, 7, g)
        if g < 3:
            query(g + 1)
    for g in range(4):
        start_out(g)
    own_mask()
    def each_head(step):
        def body(g, carry):
            step(g)
            return carry

        lax.fori_loop(0, 4, body, 0)

    @each_head
    def _(g):
        arrived(1, g)
        send(x < ROW - 1, 2, g)

        @pl.when(g == 3)
        def _():
            y5(g).start()

        arrived(3, g)
        send(first & (g > 0), 6, g)
        attend_own(g)

    @each_head
    def _(g):
        arrived(8, g)
        send(last & (g < 3), 5, g)
        send(x > 0, 7, g)
        attend(4, 1, g)

    @each_head
    def _(g):
        arrived(5, g)
        send(last, 2, g)
        arrived(7, g)
        send((x > 0) & (g > 0), 6, g)
        attend(3, 8, g)

    @each_head
    def _(g):
        arrived(2, g)

        @pl.when(g == 0)
        def _():
            y6(g).start()

        attend(5, 7, g)

    def give(n):
        return pltpu.make_async_remote_copy(
            src_ref=PP.at[n, other], dst_ref=PR.at[n], send_sem=ps.at[n], recv_sem=pr.at[n],
            device_id={"kv": other, "seq": s}, device_id_type=MESH,
        )

    def finish(n):
        give(n).wait_recv()
        cols = pl.ds(n * 512, 512)
        y = PP[n, kv] + PR[n]
        attn_ref[:, cols] = y.astype(bf16)
        mixed_ref[:, cols] = (X[kv, :, cols].astype(f32) + y).astype(bf16)

    def head_out(g):
        return jnp.concatenate([
            (ACC[g, pl.ds(h * 256, 256), :] / L[g, pl.ds(h * 256, 256), :]).astype(bf16)
            for h in range(4)], axis=1)

    def head_part(a, g, n):
        load_out(g, n).wait()
        return jnp.dot(
            a, W[2 * g + n // 4, pl.ds((n % 4) * 512, 512), :], preferred_element_type=f32)

    def settle(i, carry):
        g = lax.rem(i + 1, 3)
        arrived(6, g)
        attend(2, 6, g)
        a = head_out(g)
        for n in range(8):
            part = head_part(a, g, n)
            for r in range(2):
                half = part[r * 128:(r + 1) * 128]
                PP[n, r] = PP[n, r] + half
        return carry

    lax.fori_loop(0, 3, settle, 0)
    arrived(6, 3)
    attend(2, 6, 3)
    a = head_out(3)
    for n in range(8):
        part = head_part(a, 3, n)
        for r in range(2):
            PP[n, r] = PP[n, r] + part[r * 128:(r + 1) * 128]
        give(n).start()
        if n >= 2:
            finish(n - 2)
    finish(6)
    finish(7)

    swap.wait_send()
    for g in range(4):
        for f in relay.values():
            f(g).wait_send()
    for n in range(8):
        give(n).wait_send()
    for cp in page_copies:
        cp.wait()


def shards(n_seq, tokens, gain, w_query, w_key, w_value, w_out, segment_ids, page_table):
    bf16, f32 = jnp.bfloat16, jnp.float32
    any_spec = pl.BlockSpec(memory_space=pl.ANY)
    vmem_spec = pl.BlockSpec(memory_space=pltpu.VMEM)
    dma = pltpu.SemaphoreType.DMA
    mixed, attn_out, pages = pl.pallas_call(
        functools.partial(kernel, n_seq),
        out_shape=(
            pltpu.VMEM((128, 4096), bf16),
            pltpu.VMEM((128, 4096), bf16),
            pltpu.VMEM((2, 2, 4, 128, 128), bf16),
        ),
        in_specs=[any_spec, vmem_spec, any_spec, any_spec, any_spec, any_spec, vmem_spec],
        out_specs=(vmem_spec, vmem_spec, vmem_spec),
        scratch_shapes=[
            pltpu.VMEM((2, 128, 4096), bf16),
            pltpu.VMEM((256, 4096), bf16),
            pltpu.VMEM((12, 2048, 512), bf16),
            pltpu.VMEM((REACH + 1, 4, 2, 256, 128), bf16),
            pltpu.VMEM((4, 1024, 128), bf16),
            pltpu.VMEM((4, 1024, 128), f32),
            pltpu.VMEM((4, 1024, 128), f32),
            pltpu.VMEM((4, 1024, 128), f32),
            pltpu.VMEM((256, 256), f32),
            pltpu.VMEM((256, 128), f32),
            pltpu.VMEM((256, 128), bf16),
            pltpu.VMEM((REACH + 1, 256, 128), bf16),
            pltpu.VMEM((8, 2, 128, 512), f32),
            pltpu.VMEM((8, 128, 512), f32),
            dma((44,)), dma, dma, dma,
            dma((8, 4)), dma((REACH + 1, 4)),
            dma((8,)), dma((8,)), dma((16,)),
        ],
        compiler_params=pltpu.CompilerParams(
            collective_id=0, has_side_effects=True, vmem_limit_bytes=56 * 1024 * 1024
        ),
    )(tokens, gain.reshape(1, 4096), w_query, w_key, w_value, w_out, segment_ids.reshape(256, 128))
    page_pool = jnp.where(page_table[0] == 0, pages, pages[::-1])
    return mixed, attn_out, page_pool


def solution(mesh):
    in_specs = (
        P(("seq", "kv"), None),
        P(),
        P(None, "kv"),
        P(None, "kv"),
        P(None, "kv"),
        P("kv", None),
        P(),
        P("seq"),
    )
    out_specs = (P(("seq", "kv"), None), P(("seq", "kv"), None), P("seq", None, "kv", None, None))
    return jax.shard_map(
        functools.partial(shards, mesh.shape["seq"]),
        mesh=mesh, in_specs=in_specs, out_specs=out_specs, check_vma=False,
    )
```

time: 87.1 us -> 81.1 us (0.931)
  local copies, waits for them, and re-layouts: 4.58 us -> 1.95 us
  Pallas kernels: 79.5 us -> 77.5 us
  other arithmetic: 2.14 us -> 0.91 us
    unnamed x4, local copies, waits for them, and re-layouts: 4.58 us -> 1.95 us
    pallas_call x1, Pallas kernels: 79.5 us -> 77.5 us  [shards(): pl.pallas_call(functools.partial(kernel, n_seq), out_shape=(pltpu.VMEM((1...]
    select_n x1, other arithmetic: 2.14 us -> 0.91 us  [shards(): page_pool = jnp.where(page_table[0] == 0, pages, pages[::-1])]
where the time goes in v2:
time: 81.1 us; the launch traced here: 81 us
  Pallas kernels  77.5 us (96%)
  local copies, waits for them, and re-layouts  1.95 us (2%)
  other arithmetic  0.91 us (1%)
    pallas_call x1, Pallas kernels, shards(): pl.pallas_call(functools.partial(kernel, n_seq), out_shape=(pltpu.VMEM((1...  77.5 us
    unnamed x4, local copies, waits for them, and re-layouts  1.95 us

profile of v2, /device:TPU:1, one launch (start us, length us, event | category | flops | bytes accessed | tf_op | source)
XLA Modules:
  0.0 81.0 jit_solution(2667220488168585224)
XLA Ops:
  0.6 0.0 copy-start
  0.6 77.5 %shard_map.103 = (bf16[128,4096]{1,0:T(8,128)(2,1)S(1)}, bf16[128,4096]{1,0:T(8,128)(2,1)S(1)}, bf16[2,2,4,128,128]{4,3,2,1,0:T(8,128)(2,1)S(1)}) custom-call(bf16[128,4096]{1,0:T(8,128)(2,1)} %tok_hbm.1, f32[1,4096]{1,0:T(1,128)} %bitcast.5, bf16[4096,2048]{1,0:T(8,128)(2,1)} %wq_hbm.1, bf16[4096,512]{1,0:T(8,128)(2,1)} %wk_hbm.1, ...), custom_call_target="tpu_custom_call" | custom-call | tf_op jit(solution)/shard_map/pallas_call | solution.py:378
  78.1 1.0 %copy.13 = bf16[128,4096]{1,0:T(8,128)(2,1)} copy(bf16[128,4096]{1,0:T(8,128)(2,1)S(1)} %get-tuple-element.9) | data formatting | bytes 2097152
  79.1 1.0 %copy.14 = bf16[128,4096]{1,0:T(8,128)(2,1)} copy(bf16[128,4096]{1,0:T(8,128)(2,1)S(1)} %get-tuple-element.10) | data formatting | bytes 2097152
  80.0 0.0 copy-done
  80.1 0.9 %reverse_select_fusion = bf16[2,2,4,128,128]{4,3,2,1,0:T(8,128)(2,1)} fusion(bf16[2,2,4,128,128]{4,3,2,1,0:T(8,128)(2,1)S(1)} %get-tuple-element.8, pred[]{:T(512)} %bitcast.2), kind=kLoop, calls=%fused_computation | loop fusion | flops 262144 | bytes 1048577 | tf_op jit(solution)/shard_map/jit(_where)/select_n | solution.py:410
Async XLA Ops:
  0.6 79.4 %copy-start = (s32[2]{0:T(128)S(1)}, s32[2]{0:T(128)}, u32[]{:S(2)}) copy-start(s32[2]{0:T(128)} %param.15) | copy-start | bytes 28
